TPU v7x, 512 devices: a whole 4x4x16 slice. The times are simulated.
512 devices in a mesh: seq: 64 (over z, y), exp: 8 (over x, core).
Axes of the slice: x: 4, y: 4, z: 16, core: 2. Of those that a mesh axis runs over, the one named last changes fastest.
Arguments:
- queries: bfloat16 [16384, 6144], P('seq', 'exp'), may hold values from -6 to 6
- keys: bfloat16 [16384, 6144], P('seq', 'exp'), may hold values from -6 to 6
- values: bfloat16 [16384, 6144], P('seq', 'exp'), may hold values from -6 to 6
- selections: int32 [64, 8, 5], P('seq'), may hold values from 0 to 255
- router: bfloat16 [6144, 8], P(None, 'exp'), may hold values from -0.0390625 to 0.0390625
- w_up: bfloat16 [8, 9216, 6144], P('exp', 'seq'), may hold values from -0.15625 to 0.15625
- w_down: bfloat16 [8, 6144, 9216], P('exp', 'seq'), may hold values from -0.125 to 0.125
Outputs:
- layer_out: bfloat16 [16384, 6144], P('seq', 'exp')
Inputs may be any that keep to these rules, and one draw needn't show every extreme that they name: `selections`: entries are positions inside the block of 256 tokens; different experts may pick the same token and an expert may pick a token twice.
All inputs are finite; a program needn't handle non-finite values.
Results may differ from a plain program's by a relative error of at most 0.018.
Values may be sent and summed in bfloat16 or wider, within the bound.
No kernel may reach another device: no remote copies, remote signals or barrier semaphores. Data moves between devices by JAX's collectives and lax.ppermute only.
A program may use at most 128 MiB of HBM per device.

v0:
```python
import jax
import jax.numpy as jnp
from jax import lax
from jax.sharding import PartitionSpec as P

HEAD = 96


def entering(array, axis, join, neutral):
    place = lax.axis_index(axis)
    gathered = lax.all_gather(array.astype(jnp.bfloat16), axis)
    state = jnp.zeros_like(array) + jnp.asarray(neutral, array.dtype)

    def one(lap, state):
        return join(state, lax.dynamic_index_in_dim(gathered, lap, 0, False).astype(array.dtype))

    return lax.fori_loop(0, place, one, state)


def body(queries, keys, values, selections, router, w_up, w_down):
    length = queries.shape[0]
    width = queries.shape[1]
    heads_here = width // HEAD
    query_heads = queries.reshape(length, heads_here, HEAD)
    key_heads = keys.reshape(length, heads_here, HEAD)
    value_heads = values.reshape(length, heads_here, HEAD)
    state = jnp.einsum(
        "lhd,lhe->hde", key_heads, value_heads, preferred_element_type=jnp.float32
    ).astype(jnp.bfloat16)
    flat_size = heads_here * HEAD * HEAD
    flat_state = state.reshape(1, flat_size).astype(jnp.float32)
    empty_state = jnp.zeros((1, flat_size), jnp.float32)

    def combine_sum(earlier, later):
        return earlier + later

    before = entering(flat_state, "seq", combine_sum, empty_state)
    before = before.astype(jnp.bfloat16).reshape(heads_here, HEAD, HEAD)
    causal = jnp.arange(length)[:, None] >= jnp.arange(length)[None, :]
    scores = jnp.einsum("qhd,khd->hqk", query_heads, key_heads, preferred_element_type=jnp.float32)
    scores = jnp.where(causal[None], scores, 0.0).astype(jnp.bfloat16)
    inner = jnp.einsum("hqk,khe->qhe", scores, value_heads, preferred_element_type=jnp.float32)
    outer = jnp.einsum("qhd,hde->qhe", query_heads, before, preferred_element_type=jnp.float32)
    mixed = inner + outer
    power = jnp.mean(mixed * mixed, axis=-1, keepdims=True)
    attn = (mixed * lax.rsqrt(power + 1e-06)).astype(jnp.bfloat16).reshape(length, width)
    experts = selections.shape[1]
    capacity = selections.shape[2]
    where = selections[0].reshape(-1)
    picked = attn[where].reshape(experts, capacity, width)
    up_matrix = w_up[0]
    down_matrix = w_down[0]
    arrived = lax.all_to_all(picked, "exp", split_axis=0, concat_axis=2, tiled=True)
    own_rows = arrived.reshape(capacity, -1)
    hidden = jax.nn.silu(
        jnp.einsum(
            "rd,fd->rf",
            lax.all_gather(own_rows, "seq", axis=0, tiled=True),
            up_matrix,
            preferred_element_type=jnp.float32,
        )
    ).astype(jnp.bfloat16)
    gate_value = jax.nn.sigmoid(jnp.dot(own_rows, router, preferred_element_type=jnp.float32))
    columns = jnp.einsum(
        "rf,cf->rc",
        lax.all_gather(hidden, "seq", axis=1, tiled=True),
        down_matrix,
        preferred_element_type=jnp.float32,
    )
    expert_out = lax.all_to_all(columns, "seq", split_axis=0, concat_axis=1, tiled=True)
    weighted = (gate_value * expert_out).astype(jnp.bfloat16).reshape(1, capacity, -1)
    back = lax.all_to_all(weighted, "exp", split_axis=2, concat_axis=0, tiled=True)
    placing = (where[None, :] == jnp.arange(length, dtype=jnp.int32)[:, None]).astype(jnp.bfloat16)
    added = jnp.dot(
        placing, back.reshape(experts * capacity, width), preferred_element_type=jnp.float32
    )
    return (attn.astype(jnp.float32) + added).astype(jnp.bfloat16)


def solution(mesh):
    placed = (
        P("seq", "exp"),
        P("seq", "exp"),
        P("seq", "exp"),
        P("seq", None, None),
        P(None, "exp"),
        P("exp", "seq", None),
        P("exp", "seq", None),
    )
    return jax.shard_map(
        body, mesh=mesh, in_specs=placed, out_specs=P("seq", "exp"), check_vma=False
    )
```

profile of v0, /device:TPU:1, one launch (start us, length us, event | category | flops | bytes accessed | tf_op | source)
XLA Modules:
  0.0 761.9 jit_solution(10522953082573374514)
XLA Ops:
  6.5 0.0 copy-start
  6.5 0.0 copy-start.5
  6.5 0.0 all-gather.5.cloned.1.call-start
  6.5 1.3 copy.44
  7.9 1.2 copy.45
  9.0 0.3 convolution_convert_fusion
  9.3 1.0 all_gather.12
  10.3 0.0 all-gather.5.cloned.1.call-update
  10.3 0.0 all-gather.9.cloned.1.call-start
  10.4 1.2 copy.43
  11.5 0.0 copy-done.5
  11.5 0.1 copy.48
  11.6 0.1 reshape_squeeze.3
  11.8 209.9 %all-gather.5.cloned.1.call-done = bf16[64,1,73728]{2,1,0:T(2,128)(2,1)} async-done(((bf16[1,1,73728]{2,1,0:T(2,128)(2,1)}), bf16[64,1,73728]{2,1,0:T(2,128)(2,1)}) %all-gather.5.cloned.1.call-update) | async-done | bytes 9437200 | tf_op jit(solution)/shard_map/all_gather | solution.py:11
  221.7 0.2 broadcast_in_dim.23
  221.9 0.8 convert_reduce_fusion
  222.6 0.2 reshape.138
  222.8 1.2 convolution_bitcast_fusion
  224.0 2.8 multiply_reduce_fusion
  226.8 1.2 multiply_convert_fusion
  228.0 0.2 copy.47
  228.2 0.0 copy-start.2
  228.2 0.6 gather_fusion
  228.9 10.2 %all_to_all.46 = bf16[8,5,768]{2,1,0:T(8,128)(2,1)} all-to-all(bf16[8,5,768]{2,1,0:T(8,128)(2,1)S(1)} %reshape.140), channel_id=1, replica_groups=mesh['seq'=64,'exp'=8] {'exp'}, dimensions={0} | all-to-all | bytes 122880 | tf_op jit(solution)/shard_map/all_to_all | solution.py:53
  239.1 0.0 all-gather.9.cloned.1.call-update
  239.1 0.2 all-gather.7.cloned.1.call-start
  239.4 225.6 %all-gather.9.cloned.1.call-done = bf16[64,5,6144]{2,1,0:T(8,128)(2,1)} async-done(((bf16[1,5,6144]{2,1,0:T(8,128)(2,1)}), bf16[64,5,6144]{2,1,0:T(8,128)(2,1)}) %all-gather.9.cloned.1.call-update) | async-done | bytes 3932176 | tf_op jit(solution)/shard_map/all_gather | solution.py:58
  465.0 7.7 %reshape.154 = bf16[320,6144]{1,0:T(8,128)(2,1)} reshape(bf16[64,5,6144]{2,1,0:T(8,128)(2,1)} %all-gather.9.cloned.1.call-done) | data formatting | bytes 7864320
  472.7 0.0 copy-done.2
  472.7 0.0 copy-done
  472.7 4.3 multiply_convert_fusion.1
  477.0 0.0 all-gather.7.cloned.1.call-update
  477.0 148.1 %all-gather.7.cloned.1.call-done = bf16[320,9216]{0,1:T(8,128)(2,1)} async-done(((bf16[320,144]{0,1:T(8,128)(2,1)}), bf16[320,9216]{0,1:T(8,128)(2,1)}) %all-gather.7.cloned.1.call-update) | async-done | bytes 5898256 | tf_op jit(solution)/shard_map/all_gather | solution.py:66
  625.1 9.3 %copy.51 = bf16[320,9216]{1,0:T(8,128)(2,1)} copy(bf16[320,9216]{0,1:T(8,128)(2,1)} %all-gather.7.cloned.1.call-done) | data formatting | bytes 11796480 | tf_op jit(solution)/shard_map/all_gather | solution.py:66
  634.4 9.2 %dot_general.32 = bf16[64,5,9216]{2,1,0:T(8,128)(2,1)} reshape(bf16[320,9216]{1,0:T(8,128)(2,1)} %copy.51) | data formatting | bytes 11796480 | tf_op jit(solution)/shard_map/rf,cf->rc/dot_general | solution.py:64
  643.6 0.0 copy-start.4
  643.6 0.0 copy-start.6
  643.6 10.6 %fusion = f32[64,5,96]{2,0,1:T(8,128)S(1)} fusion(bf16[64,5,9216]{2,1,0:T(8,128)(2,1)} %dot_general.32, bf16[1,96,9216]{2,1,0:T(8,128)(2,1)} %param.15), kind=kOutput, calls=%fused_computation.2 | convolution fusion | flops 566231040 | bytes 7790592 | tf_op jit(solution)/shard_map/rf,cf->rc/dot_general | solution.py:64
  654.2 0.1 copy.53
  654.3 0.9 reshape.161
  655.2 9.4 %all-to-all-start.1 = ((f32[64,1,480]{2,1,0:T(1,128)}), f32[64,1,480]{2,1,0:T(1,128)S(1)}, u32[]{:S(2)}, u32[]{:S(2)}) async-start(f32[64,1,480]{2,1,0:T(1,128)} %reshape.161), calls=%async_computation.1 | async-start | bytes 262144 | tf_op jit(solution)/shard_map/all_to_all | solution.py:70
  664.5 0.0 copy-done.4
  664.6 0.0 copy-done.6
  664.6 0.2 fusion.12
  664.7 14.7 %all-to-all-done.1 = f32[64,1,480]{2,1,0:T(1,128)S(1)} async-done(((f32[64,1,480]{2,1,0:T(1,128)}), f32[64,1,480]{2,1,0:T(1,128)S(1)}, u32[]{:S(2)}, u32[]{:S(2)}) %all-to-all-start.1) | async-done | bytes 122912 | tf_op jit(solution)/shard_map/all_to_all | solution.py:70
  679.4 0.5 broadcast.59
  680.0 0.9 reduce.2
  680.9 0.1 reshape.162
  681.0 0.1 all_to_all.39
  681.2 0.1 multiply_convert_fusion.2
  681.3 5.2 copy.55
  686.5 0.5 broadcast.60
  687.0 34.2 %reduce.3 = bf16[6144,5]{1,0:T(8,128)(2,1)S(1)} reduce(bf16[6144,1,5]{2,1,0:T(2,128)(2,1)} %bitcast.68, bf16[]{:T(256)} %broadcast.60), dimensions={1}, to_apply=%bitcast.51.reduce_sub_computation | reduce | bytes 122882
  721.2 0.0 copy-start.1
  721.2 3.0 reshape.163
  724.3 0.0 copy-start.3
  724.3 14.1 %all-to-all-start.2 = ((bf16[8,2,1920]{2,1,0:T(2,128)(2,1)}), bf16[8,2,1920]{2,1,0:T(2,128)(2,1)S(1)}, u32[]{:S(2)}, u32[]{:S(2)}) async-start(bf16[8,2,1920]{2,1,0:T(2,128)(2,1)} %reshape.163), calls=%async_computation.2 | async-start | bytes 122880 | tf_op jit(solution)/shard_map/all_to_all | solution.py:72
  738.4 0.1 eq.15
  738.4 4.8 all-to-all-done.2
  743.2 5.1 reshape.164
  748.3 6.0 copy.56
  754.4 0.0 copy-done.3
  754.4 1.0 fusion.8
  755.4 0.0 copy-done.1
  (10 shorter events, 0.2 us)
Async XLA Ops:
  6.5 466.1 %copy-start = (bf16[1,144,6144]{2,1,0:T(8,128)(2,1)S(1)}, bf16[1,144,6144]{2,1,0:T(8,128)(2,1)}, u32[]{:S(2)}) copy-start(bf16[1,144,6144]{2,1,0:T(8,128)(2,1)} %param.14) | copy-start | bytes 5308420
  6.5 5.0 copy-start.5
  6.5 215.2 %all-gather.5.cloned.1.call-start = ((), (), s32[]{:S(2)}) async-start(), calls=%async_computation.3 | async-start | bytes 19169280 | tf_op jit(solution)/shard_map/all_gather | solution.py:11
  10.3 454.7 %all-gather.9.cloned.1.call-start = ((), (), s32[]{:S(2)}) async-start(), calls=%async_computation.5 | async-start | bytes 6389760 | tf_op jit(solution)/shard_map/all_gather | solution.py:58
  228.2 244.5 %copy-start.2 = (bf16[256,768]{1,0:T(8,128)(2,1)}, bf16[256,768]{1,0:T(8,128)(2,1)S(1)}, u32[]{:S(2)}) copy-start(bf16[256,768]{1,0:T(8,128)(2,1)S(1)} %copy.47) | copy-start | bytes 1179652
  239.1 386.0 %all-gather.7.cloned.1.call-start = ((), (), s32[]{:S(2)}) async-start(), calls=%async_computation.4 | async-start | bytes 7188480 | tf_op jit(solution)/shard_map/all_gather | solution.py:66
  643.6 21.0 %copy-start.4 = (bf16[8,5,768]{2,1,0:T(8,128)(2,1)S(1)}, bf16[8,5,768]{2,1,0:T(8,128)(2,1)}, u32[]{:S(2)}) copy-start(bf16[8,5,768]{2,1,0:T(8,128)(2,1)} %all_to_all.46) | copy-start | bytes 184324
  643.6 21.0 %copy-start.6 = (bf16[6144,1]{0,1:T(2,128)(2,1)S(1)}, bf16[6144,1]{0,1:T(2,128)(2,1)}, u32[]{:S(2)}) copy-start(bf16[6144,1]{0,1:T(2,128)(2,1)} %param.13) | copy-start | bytes 36868
  655.2 24.2 %all-to-all-start.1 = ((f32[64,1,480]{2,1,0:T(1,128)}), f32[64,1,480]{2,1,0:T(1,128)S(1)}, u32[]{:S(2)}, u32[]{:S(2)}) async-start(f32[64,1,480]{2,1,0:T(1,128)} %reshape.161), calls=%async_computation.1 | async-start | bytes 262144 | tf_op jit(solution)/shard_map/all_to_all | solution.py:70
  721.2 34.1 %copy-start.1 = (bf16[1,144,6144]{2,1,0:T(8,128)(2,1)S(1)}, bf16[1,144,6144]{2,1,0:T(8,128)(2,1)}, u32[]{:S(2)}) copy-start(bf16[1,144,6144]{2,1,0:T(8,128)(2,1)} %param.14) | copy-start | bytes 5308420
  724.3 30.1 %copy-start.3 = (bf16[256,768]{1,0:T(8,128)(2,1)S(1)}, bf16[256,768]{1,0:T(8,128)(2,1)}, u32[]{:S(2)}) copy-start(bf16[256,768]{1,0:T(8,128)(2,1)} %copy-done.2) | copy-start | bytes 1179652
  724.3 18.9 %all-to-all-start.2 = ((bf16[8,2,1920]{2,1,0:T(2,128)(2,1)}), bf16[8,2,1920]{2,1,0:T(2,128)(2,1)S(1)}, u32[]{:S(2)}, u32[]{:S(2)}) async-start(bf16[8,2,1920]{2,1,0:T(2,128)(2,1)} %reshape.163), calls=%async_computation.2 | async-start | bytes 122880 | tf_op jit(solution)/shard_map/all_to_all | solution.py:72
Sparse Core Ops, SparseCore 0:
  10.4 211.2 all-gather.4
  239.3 225.6 all-gather.8
  477.2 147.9 all-gather.6
where the time goes:
time: 765 us; the launch traced here: 762 us
  waiting for transfers between devices  603 us (79%)
  local copies, waits for them, and re-layouts  53.9 us (7%)
  other arithmetic  37.3 us (5%)
  starting transfers between devices  23.7 us (3%)
  matrix products  20.3 us (3%)
  between operations  13.3 us (2%)
  blocking collectives  10.2 us (1%)
    all_gather x1, waiting for transfers between devices, body(): lax.all_gather(own_rows, 'seq', axis=0, tiled=True)  226 us
    all_gather x1, waiting for transfers between devices, entering(): gathered = lax.all_gather(array.astype(jnp.bfloat16), axis)  210 us
    all_gather x1, waiting for transfers between devices, body(): lax.all_gather(hidden, 'seq', axis=1, tiled=True)  148 us
    unnamed x1, other arithmetic  34.2 us
    unnamed x25, local copies, waits for them, and re-layouts  21 us
  transfers between devices with their start and end apart: 5, of which 5 were waited for; matrix products, arithmetic and copies ran while one was open for 0% of the time, Pallas kernels for 0%

commit v1 on v0

--- a/solution.py
+++ b/solution.py
@@ -69,7 +69,9 @@
     )
     expert_out = lax.all_to_all(columns, "seq", split_axis=0, concat_axis=1, tiled=True)
     weighted = (gate_value * expert_out).astype(jnp.bfloat16).reshape(1, capacity, -1)
-    back = lax.all_to_all(weighted, "exp", split_axis=2, concat_axis=0, tiled=True)
+    pieces = jnp.split(weighted, lax.axis_size("exp"), axis=2)
+    arrived_2 = lax.all_to_all(jnp.stack(pieces), "exp", 0, 0)
+    back = jnp.concatenate(arrived_2, axis=0)
     placing = (where[None, :] == jnp.arange(length, dtype=jnp.int32)[:, None]).astype(jnp.bfloat16)
     added = jnp.dot(
         placing, back.reshape(experts * capacity, width), preferred_element_type=jnp.float32

time: 765 us -> 716 us (0.936)
  other arithmetic: 37.3 us -> 3.06 us
  local copies, waits for them, and re-layouts: 53.9 us -> 38.8 us
    unnamed x1 -> x0, other arithmetic: 34.2 us -> none
    unnamed x25 -> x22, local copies, waits for them, and re-layouts: 21 us -> 16.6 us
where the time goes in v1:
time: 716 us; the launch traced here: 713 us
  waiting for transfers between devices  604 us (84%)
  local copies, waits for them, and re-layouts  38.8 us (5%)
  starting transfers between devices  23.4 us (3%)
  matrix products  20.3 us (3%)
  between operations  13.3 us (2%)
  blocking collectives  10.2 us (1%)
    all_gather x1, waiting for transfers between devices, body(): lax.all_gather(own_rows, 'seq', axis=0, tiled=True)  226 us
    all_gather x1, waiting for transfers between devices, entering(): gathered = lax.all_gather(array.astype(jnp.bfloat16), axis)  210 us
    all_gather x1, waiting for transfers between devices, body(): lax.all_gather(hidden, 'seq', axis=1, tiled=True)  148 us
    unnamed x22, local copies, waits for them, and re-layouts  16.6 us
    all_to_all x1, waiting for transfers between devices, body(): lax.all_to_all(columns, 'seq', split_axis=0, concat_axis=1, tiled=True)  14.9 us
  transfers between devices with their start and end apart: 5, of which 5 were waited for; matrix products, arithmetic and copies ran while one was open for 0% of the time, Pallas kernels for 0%

profile of v1, /device:TPU:1, one launch (start us, length us, event | category | flops | bytes accessed | tf_op | source)
XLA Modules:
  0.0 712.6 jit_solution(10451731566077537861)
XLA Ops:
  6.5 0.0 copy-start
  6.5 0.0 copy-start.2
  6.5 0.0 all-gather.5.cloned.1.call-start
  6.5 1.3 copy.29
  7.9 1.2 copy.30
  9.0 0.3 convolution_convert_fusion
  9.3 1.0 all_gather.12
  10.3 0.0 all-gather.5.cloned.1.call-update
  10.3 0.0 all-gather.9.cloned.1.call-start
  10.4 1.2 copy.28
  11.5 0.0 copy-done.2
  11.5 0.1 copy.33
  11.6 0.1 reshape_squeeze.3
  11.8 209.9 %all-gather.5.cloned.1.call-done = bf16[64,1,73728]{2,1,0:T(2,128)(2,1)} async-done(((bf16[1,1,73728]{2,1,0:T(2,128)(2,1)}), bf16[64,1,73728]{2,1,0:T(2,128)(2,1)}) %all-gather.5.cloned.1.call-update) | async-done | bytes 9437200 | tf_op jit(solution)/shard_map/all_gather | solution.py:11
  221.7 0.2 broadcast_in_dim.23
  221.9 0.8 convert_reduce_fusion
  222.6 0.2 reshape.134
  222.8 1.2 convolution_bitcast_fusion
  224.0 2.8 multiply_reduce_fusion
  226.8 1.2 multiply_convert_fusion
  228.0 0.2 copy.32
  228.2 0.6 gather_fusion
  228.9 10.2 %all_to_all.36 = bf16[8,5,768]{2,1,0:T(8,128)(2,1)} all-to-all(bf16[8,5,768]{2,1,0:T(8,128)(2,1)S(1)} %reshape.136), channel_id=1, replica_groups=mesh['seq'=64,'exp'=8] {'exp'}, dimensions={0} | all-to-all | bytes 122880 | tf_op jit(solution)/shard_map/all_to_all | solution.py:53
  239.1 0.0 all-gather.9.cloned.1.call-update
  239.1 0.2 all-gather.7.cloned.1.call-start
  239.4 225.6 %all-gather.9.cloned.1.call-done = bf16[64,5,6144]{2,1,0:T(8,128)(2,1)} async-done(((bf16[1,5,6144]{2,1,0:T(8,128)(2,1)}), bf16[64,5,6144]{2,1,0:T(8,128)(2,1)}) %all-gather.9.cloned.1.call-update) | async-done | bytes 3932176 | tf_op jit(solution)/shard_map/all_gather | solution.py:58
  465.0 7.7 %reshape.149 = bf16[320,6144]{1,0:T(8,128)(2,1)} reshape(bf16[64,5,6144]{2,1,0:T(8,128)(2,1)} %all-gather.9.cloned.1.call-done) | data formatting | bytes 7864320
  472.7 0.0 copy-done
  472.7 4.3 multiply_convert_fusion.1
  477.0 0.0 all-gather.7.cloned.1.call-update
  477.0 148.1 %all-gather.7.cloned.1.call-done = bf16[320,9216]{0,1:T(8,128)(2,1)} async-done(((bf16[320,144]{0,1:T(8,128)(2,1)}), bf16[320,9216]{0,1:T(8,128)(2,1)}) %all-gather.7.cloned.1.call-update) | async-done | bytes 5898256 | tf_op jit(solution)/shard_map/all_gather | solution.py:66
  625.2 9.3 %copy.36 = bf16[320,9216]{1,0:T(8,128)(2,1)} copy(bf16[320,9216]{0,1:T(8,128)(2,1)} %all-gather.7.cloned.1.call-done) | data formatting | bytes 11796480 | tf_op jit(solution)/shard_map/all_gather | solution.py:66
  634.4 9.2 %dot_general.32 = bf16[64,5,9216]{2,1,0:T(8,128)(2,1)} reshape(bf16[320,9216]{1,0:T(8,128)(2,1)} %copy.36) | data formatting | bytes 11796480 | tf_op jit(solution)/shard_map/rf,cf->rc/dot_general | solution.py:64
  643.6 0.0 copy-start.1
  643.6 0.0 copy-start.3
  643.6 10.6 %fusion = f32[64,5,96]{2,0,1:T(8,128)S(1)} fusion(bf16[64,5,9216]{2,1,0:T(8,128)(2,1)} %dot_general.32, bf16[1,96,9216]{2,1,0:T(8,128)(2,1)} %param.15), kind=kOutput, calls=%fused_computation.2 | convolution fusion | flops 566231040 | bytes 7790592 | tf_op jit(solution)/shard_map/rf,cf->rc/dot_general | solution.py:64
  654.2 0.1 copy.38
  654.3 0.9 reshape.156
  655.2 9.1 %all-to-all-start.1 = ((f32[64,1,480]{2,1,0:T(1,128)}), f32[64,1,480]{2,1,0:T(1,128)S(1)}, u32[]{:S(2)}, u32[]{:S(2)}) async-start(f32[64,1,480]{2,1,0:T(1,128)} %reshape.156), calls=%async_computation.1 | async-start | bytes 262144 | tf_op jit(solution)/shard_map/all_to_all | solution.py:70
  664.3 0.0 copy-done.1
  664.4 0.0 copy-done.3
  664.4 0.2 fusion.12
  664.5 14.9 %all-to-all-done.1 = f32[64,1,480]{2,1,0:T(1,128)S(1)} async-done(((f32[64,1,480]{2,1,0:T(1,128)}), f32[64,1,480]{2,1,0:T(1,128)S(1)}, u32[]{:S(2)}, u32[]{:S(2)}) %all-to-all-start.1) | async-done | bytes 122912 | tf_op jit(solution)/shard_map/all_to_all | solution.py:70
  679.4 0.5 broadcast.59
  680.0 1.0 reduce.2
  680.9 0.1 reshape.157
  681.1 0.1 all_to_all.31
  681.2 0.1 multiply_convert_fusion.2
  681.3 0.6 constant_dynamic-update-slice_fusion.7
  681.9 0.6 constant_dynamic-update-slice_fusion.6
  682.5 0.6 constant_dynamic-update-slice_fusion.5
  683.1 0.6 constant_dynamic-update-slice_fusion.4
  683.7 0.6 constant_dynamic-update-slice_fusion.3
  684.3 0.6 constant_dynamic-update-slice_fusion.2
  684.9 0.6 constant_dynamic-update-slice_fusion.1
  685.5 0.6 constant_dynamic-update-slice_fusion
  686.1 14.0 %all-to-all-start.2 = ((bf16[8,1,5,768]{3,2,1,0:T(8,128)(2,1)}), bf16[8,1,5,768]{3,2,1,0:T(8,128)(2,1)S(1)}, u32[]{:S(2)}, u32[]{:S(2)}) async-start(bf16[8,1,5,768]{3,2,1,0:T(8,128)(2,1)} %constant_dynamic-update-slice_fusion), calls=%async_computation.2 | async-start | bytes 196608 | tf_op jit(solution)/shard_map/all_to_all | solution.py:73
  700.1 0.1 eq.15
  700.1 4.9 all-to-all-done.2
  705.1 1.0 fusion.8
  (8 shorter events, 0.2 us)
Async XLA Ops:
  6.5 466.1 %copy-start = (bf16[1,144,6144]{2,1,0:T(8,128)(2,1)S(1)}, bf16[1,144,6144]{2,1,0:T(8,128)(2,1)}, u32[]{:S(2)}) copy-start(bf16[1,144,6144]{2,1,0:T(8,128)(2,1)} %param.14) | copy-start | bytes 5308420
  6.5 5.0 copy-start.2
  6.5 215.2 %all-gather.5.cloned.1.call-start = ((), (), s32[]{:S(2)}) async-start(), calls=%async_computation.3 | async-start | bytes 19169280 | tf_op jit(solution)/shard_map/all_gather | solution.py:11
  10.3 454.7 %all-gather.9.cloned.1.call-start = ((), (), s32[]{:S(2)}) async-start(), calls=%async_computation.5 | async-start | bytes 6389760 | tf_op jit(solution)/shard_map/all_gather | solution.py:58
  239.1 386.0 %all-gather.7.cloned.1.call-start = ((), (), s32[]{:S(2)}) async-start(), calls=%async_computation.4 | async-start | bytes 7188480 | tf_op jit(solution)/shard_map/all_gather | solution.py:66
  643.6 20.8 %copy-start.1 = (bf16[8,5,768]{2,1,0:T(8,128)(2,1)S(1)}, bf16[8,5,768]{2,1,0:T(8,128)(2,1)}, u32[]{:S(2)}) copy-start(bf16[8,5,768]{2,1,0:T(8,128)(2,1)} %all_to_all.36) | copy-start | bytes 184324
  643.6 20.8 %copy-start.3 = (bf16[6144,1]{0,1:T(2,128)(2,1)S(1)}, bf16[6144,1]{0,1:T(2,128)(2,1)}, u32[]{:S(2)}) copy-start(bf16[6144,1]{0,1:T(2,128)(2,1)} %param.13) | copy-start | bytes 36868
  655.2 24.2 %all-to-all-start.1 = ((f32[64,1,480]{2,1,0:T(1,128)}), f32[64,1,480]{2,1,0:T(1,128)S(1)}, u32[]{:S(2)}, u32[]{:S(2)}) async-start(f32[64,1,480]{2,1,0:T(1,128)} %reshape.156), calls=%async_computation.1 | async-start | bytes 262144 | tf_op jit(solution)/shard_map/all_to_all | solution.py:70
  686.1 18.9 %all-to-all-start.2 = ((bf16[8,1,5,768]{3,2,1,0:T(8,128)(2,1)}), bf16[8,1,5,768]{3,2,1,0:T(8,128)(2,1)S(1)}, u32[]{:S(2)}, u32[]{:S(2)}) async-start(bf16[8,1,5,768]{3,2,1,0:T(8,128)(2,1)} %constant_dynamic-update-slice_fusion), calls=%async_computation.2 | async-start | bytes 196608 | tf_op jit(solution)/shard_map/all_to_all | solution.py:73
Sparse Core Ops, SparseCore 0:
  10.4 211.2 all-gather.4
  239.2 225.6 all-gather.8
  477.2 147.9 all-gather.6
